TPU v7x, 32 devices: a whole 2x2x4 slice. The times are simulated.
32 devices in a mesh: row: 8 (over y, x, core), col: 4 (over z).
Axes of the slice: x: 2, y: 2, z: 4, core: 2. Of those that a mesh axis runs over, the one named last changes fastest.
Arguments:
- documents: float32 [6144, 768], P('row', 'col'), may hold values from -6 to 6
- projection: float32 [768, 768], P('col'), may hold values from -0.21875 to 0.21875
- landmarks: float32 [16384, 768], P('col', 'row'), may hold values from -6 to 6
- coefficients: float32 [16384, 128], P('col'), may hold values from -6 to 6
- inverse_tiles: float32 [16384, 16384], P('col', 'row'), may hold values from -0.046875 to 0.046875
- labels: int32 [6144, 128], P('row'), may hold values 0 or 1
Outputs:
- new_coefficients: float32 [16384, 128], P('col')
- residual: float32 [6144, 128], P('row')
All inputs are finite; a program needn't handle non-finite values. No bound on the sum of `labels` on one device may be relied on, other than what follows from the above.
Results may differ from a plain program's by a relative error of at most 0.0001.
Values sent between devices are 32-bit elements; how exact they have to be, the bound alone decides.
A program may use at most 128 MiB of HBM per device.

v0:
```python
import jax
import jax.numpy as jnp
from jax import lax
from jax.sharding import PartitionSpec as P

ITERS = 2


def broadcast(block, axis, owner):
    block = jnp.where(lax.axis_index(axis) == owner, block, jnp.zeros_like(block))
    return lax.psum(block, axis)


def on_device(documents, projection, landmarks, coefficients, inverse_tiles, labels):
    highest = lax.Precision.HIGHEST
    land_full = lax.all_gather(landmarks, "row", axis=1, tiled=True)
    sq_land = jnp.sum(land_full * land_full, axis=1)
    feature_width = land_full.shape[1]
    proj_share = lax.psum_scatter(
        jnp.dot(documents, projection, precision=highest, preferred_element_type=jnp.float32),
        "col",
        scatter_dimension=0,
        tiled=True,
    )
    rows_in = lax.all_gather(proj_share, "col", axis=0, tiled=True)
    sq_doc = jnp.sum(rows_in * rows_in, axis=1)
    inner = lax.dot_general(
        rows_in,
        land_full,
        (((1,), (1,)), ((), ())),
        precision=highest,
        preferred_element_type=jnp.float32,
    )
    kernel = jnp.exp(-2.0 * (sq_doc[:, None] + sq_land[None, :] - 2.0 * inner) / feature_width)
    row_count = lax.axis_size("row")
    col_count = lax.axis_size("col")
    step_size = 64.0 / (documents.shape[0] * row_count)
    block_rows = inverse_tiles.shape[1]
    group_size = row_count // col_count
    row_index = lax.axis_index("row")
    source = row_index // group_size
    offset = row_index % group_size * block_rows
    current = coefficients
    target = labels.astype(jnp.float32)
    residual = jnp.zeros((documents.shape[0], labels.shape[1]), jnp.float32)
    for iteration in range(ITERS):
        local_pred = jnp.dot(kernel, current, precision=highest, preferred_element_type=jnp.float32)
        predicted = lax.psum(local_pred, "col")
        residual = jax.nn.sigmoid(predicted) - target
        local_grad = lax.dot_general(
            kernel,
            residual,
            (((0,), (0,)), ((), ())),
            precision=highest,
            preferred_element_type=jnp.float32,
        )
        gradient = lax.psum(local_grad, "row")
        grad_block = lax.dynamic_slice_in_dim(gradient, offset, block_rows, 0)
        grad_block = broadcast(grad_block, "col", source)
        product_term = jnp.dot(
            inverse_tiles, grad_block, precision=highest, preferred_element_type=jnp.float32
        )
        current = current - step_size * lax.psum(product_term, "row")
    return (current, residual)


def solution(mesh):
    in_specs = (
        P("row", "col"),
        P("col", None),
        P("col", "row"),
        P("col", None),
        P("col", "row"),
        P("row", None),
    )
    out_specs = (P("col", None), P("row", None))
    return jax.shard_map(
        on_device, mesh=mesh, in_specs=in_specs, out_specs=out_specs, check_vma=False
    )
```

profile of v0, /device:TPU:0, one launch (start us, length us, event | category | flops | bytes accessed | tf_op | source)
XLA Modules:
  0.0 830.2 jit_solution(13493316278043722178)
XLA Ops:
  7.2 0.0 reduce-scatter.2.cloned.1.call-start
  7.2 1.0 copy-done
  8.2 4.6 fusion.11
  12.8 0.0 all-gather.3.cloned.1.call-start
  12.9 50.5 %reduce-scatter.2.cloned.1.call-done = f32[192,768]{1,0:T(8,128)} async-done(((f32[768,768]{1,0:T(8,128)}), f32[192,768]{1,0:T(8,128)}) %reduce-scatter.2.cloned.1.call-update) | async-done | bytes 589840 | tf_op jit(solution)/shard_map/reduce_scatter | solution.py:19
  63.4 0.0 all-gather.5.cloned.1.call-start
  63.5 0.7 all-gather.5.cloned.1.call-update
  64.2 0.0 all-reduce.9.cloned.1.call-start
  64.2 50.2 %all-gather.3.cloned.1.call-done = f32[768,768]{1,0:T(8,128)} async-done(((f32[192,768]{1,0:T(8,128)}), f32[768,768]{1,0:T(8,128)}) %all-gather.3.cloned.1.call-update) | async-done | bytes 2359312 | tf_op jit(solution)/shard_map/all_gather | solution.py:25
  114.4 2.0 multiply_reduce_fusion.1
  116.4 70.6 %all-gather.5.cloned.1.call-done = f32[4096,768]{0,1:T(8,128)} async-done(((f32[4096,96]{0,1:T(8,128)}), f32[4096,768]{0,1:T(8,128)}) %all-gather.5.cloned.1.call-update) | async-done | bytes 12582928 | tf_op jit(solution)/shard_map/all_gather | solution.py:16
  187.1 5.9 multiply_reduce_fusion
  192.9 2.3 copy-done.3
  195.2 32.1 %multiply_exponential_fusion = f32[768,4096]{1,0:T(8,128)S(1)} fusion(f32[768,768]{1,0:T(8,128)S(1)} %copy-done.5, f32[4096,768]{0,1:T(8,128)S(1)} %copy-done.3, f32[4096]{0:T(1024)S(1)} %multiply_reduce_fusion, f32[768]{0:T(1024)S(1)} %multiply_reduce_fusion.1), kind=kOutput, calls=%fused_computation | convolution fusion | flops 29003612160 | bytes 27544576 | tf_op jit(solution)/shard_map/dot_general | solution.py:27
  227.4 4.5 copy-done.2
  231.9 10.6 %fusion.12 = f32[768,128]{1,0:T(8,128)} fusion(f32[768,4096]{1,0:T(8,128)S(1)} %multiply_exponential_fusion, f32[4096,128]{1,0:T(8,128)S(1)} %copy-done.4), kind=kOutput, calls=%fused_computation.22 | convolution fusion | flops 4831838208 | bytes 15073280 | tf_op jit(solution)/shard_map/dot_general | solution.py:47
  242.6 0.0 all-reduce.11.cloned.1.call-start
  242.6 37.0 %all-reduce.9.cloned.1.call-done = f32[768,128]{1,0:T(8,128)} async-done(((f32[768,128]{1,0:T(8,128)}), f32[768,128]{1,0:T(8,128)}) %all-reduce.9.cloned.1.call-update) | async-done | bytes 393232 | tf_op jit(solution)/shard_map/psum | solution.py:48
  279.7 24.0 %fusion.1 = f32[4096,128]{1,0:T(8,128)} fusion(f32[768,4096]{1,0:T(8,128)} %copy-done.2, s32[768,128]{1,0:T(8,128)S(1)} %copy-done.6, f32[768,128]{1,0:T(8,128)} %all-reduce.9.cloned.1.call-done), kind=kOutput, calls=%fused_computation.11 | convolution fusion | flops 4832329728 | bytes 15466496 | tf_op jit(solution)/shard_map/dot_general | solution.py:50
  303.7 0.0 all-reduce.11.cloned.1.call-update
  303.7 0.0 all-reduce.13.cloned.1.call-start
  303.8 61.6 %all-reduce.11.cloned.1.call-done = f32[4096,128]{1,0:T(8,128)} async-done(((f32[4096,128]{1,0:T(8,128)}), f32[4096,128]{1,0:T(8,128)}) %all-reduce.11.cloned.1.call-update) | async-done | bytes 2097168 | tf_op jit(solution)/shard_map/psum | solution.py:57
  365.4 2.3 dynamic-slice_select_fusion.1
  367.6 0.0 all-reduce.15.cloned.1.call-start
  367.7 51.5 %all-reduce.13.cloned.1.call-done = f32[2048,128]{1,0:T(8,128)} async-done(((f32[2048,128]{1,0:T(8,128)}), f32[2048,128]{1,0:T(8,128)}) %all-reduce.13.cloned.1.call-update) | async-done | bytes 1048592 | tf_op jit(solution)/shard_map/psum | solution.py:11
  419.1 42.4 %convolution_bitcast_fusion.1 = f32[4096,128]{0,1:T(8,128)} fusion(f32[2048,128]{1,0:T(8,128)} %all-reduce.13.cloned.1.call-done, f32[4096,2048]{1,0:T(8,128)} %param.10), kind=kOutput, calls=%fused_computation.3 | convolution fusion | flops 12884901888 | bytes 36700160 | tf_op jit(solution)/shard_map/dot_general | solution.py:60
  461.6 0.0 all-reduce.15.cloned.1.call-update
  461.6 0.0 all-reduce.17.cloned.1.call-start
  461.7 1.9 copy.8
  463.6 59.2 %all-reduce.15.cloned.1.call-done = f32[4096,128]{0,1:T(8,128)} async-done(((f32[4096,128]{0,1:T(8,128)}), f32[4096,128]{0,1:T(8,128)}) %all-reduce.15.cloned.1.call-update) | async-done | bytes 2097168 | tf_op jit(solution)/shard_map/psum | solution.py:63
  522.8 13.9 %fusion = f32[768,128]{1,0:T(8,128)} fusion(f32[768,4096]{1,0:T(8,128)} %copy-done.2, f32[4096,128]{0,1:T(8,128)S(1)} %copy.8, f32[4096,128]{0,1:T(8,128)} %all-reduce.15.cloned.1.call-done), kind=kOutput, calls=%fused_computation.9 | convolution fusion | flops 4832886784 | bytes 17170432 | tf_op jit(solution)/shard_map/dot_general | solution.py:47
  536.7 0.0 all-reduce.17.cloned.1.call-update
  536.7 0.0 all-reduce.19.cloned.1.call-start
  536.7 36.1 %all-reduce.17.cloned.1.call-done = f32[768,128]{1,0:T(8,128)} async-done(((f32[768,128]{1,0:T(8,128)}), f32[768,128]{1,0:T(8,128)}) %all-reduce.17.cloned.1.call-update) | async-done | bytes 393232 | tf_op jit(solution)/shard_map/psum | solution.py:48
  572.9 1.1 divide_subtract_fusion
  574.0 23.8 %fusion.13 = f32[4096,128]{1,0:T(8,128)} fusion(f32[768,4096]{1,0:T(8,128)} %copy-done.2, f32[768,128]{1,0:T(8,128)S(1)} %divide_subtract_fusion), kind=kOutput, calls=%fused_computation.23 | convolution fusion | flops 4831838208 | bytes 15073280 | tf_op jit(solution)/shard_map/dot_general | solution.py:50
  597.8 0.0 all-reduce.19.cloned.1.call-update
  597.8 0.0 all-reduce.21.cloned.1.call-start
  597.9 61.6 %all-reduce.19.cloned.1.call-done = f32[4096,128]{1,0:T(8,128)} async-done(((f32[4096,128]{1,0:T(8,128)}), f32[4096,128]{1,0:T(8,128)}) %all-reduce.19.cloned.1.call-update) | async-done | bytes 2097168 | tf_op jit(solution)/shard_map/psum | solution.py:57
  659.5 2.3 dynamic-slice_select_fusion
  661.8 0.0 all-reduce.21.cloned.1.call-update
  661.8 0.0 all-reduce.23.cloned.1.call-start
  661.9 51.4 %all-reduce.21.cloned.1.call-done = f32[2048,128]{1,0:T(8,128)} async-done(((f32[2048,128]{1,0:T(8,128)}), f32[2048,128]{1,0:T(8,128)}) %all-reduce.21.cloned.1.call-update) | async-done | bytes 1048592 | tf_op jit(solution)/shard_map/psum | solution.py:11
  713.3 42.0 %convolution_bitcast_fusion = f32[4096,128]{0,1:T(8,128)} fusion(f32[2048,128]{1,0:T(8,128)} %all-reduce.21.cloned.1.call-done, f32[4096,2048]{1,0:T(8,128)} %param.10), kind=kOutput, calls=%fused_computation.2 | convolution fusion | flops 12884901888 | bytes 36700160 | tf_op jit(solution)/shard_map/dot_general | solution.py:60
  755.3 0.0 all-reduce.23.cloned.1.call-update
  755.4 61.2 %all-reduce.23.cloned.1.call-done = f32[4096,128]{0,1:T(8,128)} async-done(((f32[4096,128]{0,1:T(8,128)}), f32[4096,128]{0,1:T(8,128)}) %all-reduce.23.cloned.1.call-update) | async-done | bytes 2097168 | tf_op jit(solution)/shard_map/psum | solution.py:63
  816.5 4.0 multiply_subtract_fusion
  820.6 2.9 copy.9
  (17 shorter events, 0.1 us)
Async XLA Ops:
  7.2 1.1 copy-start
  7.2 56.2 %reduce-scatter.2.cloned.1.call-start = ((), (), s32[]{:S(2)}) async-start(), calls=%async_computation.1 | async-start | bytes 2949120 | tf_op jit(solution)/shard_map/reduce_scatter | solution.py:19
  12.8 101.5 %all-gather.3.cloned.1.call-start = ((), (), s32[]{:S(2)}) async-start(), calls=%async_computation.2 | async-start | bytes 2949120 | tf_op jit(solution)/shard_map/all_gather | solution.py:25
  63.4 123.6 %all-gather.5.cloned.1.call-start = ((), (), s32[]{:S(2)}) async-start(), calls=%async_computation.3 | async-start | bytes 14155776 | tf_op jit(solution)/shard_map/all_gather | solution.py:16
  64.2 215.5 %all-reduce.9.cloned.1.call-start = ((), (), s32[]{:S(2)}) async-start(), calls=%async_computation.4 | async-start | bytes 786432 | tf_op jit(solution)/shard_map/psum | solution.py:48
  114.4 78.6 %copy-start.5 = (f32[768,768]{1,0:T(8,128)S(1)}, f32[768,768]{1,0:T(8,128)}, u32[]{:S(2)}) copy-start(f32[768,768]{1,0:T(8,128)} %all-gather.3.cloned.1.call-done) | copy-start | bytes 7077892
  187.1 8.2 copy-start.3
  195.2 36.7 %copy-start.4 = (f32[4096,128]{1,0:T(8,128)S(1)}, f32[4096,128]{1,0:T(8,128)}, u32[]{:S(2)}) copy-start(f32[4096,128]{1,0:T(8,128)} %param.9) | copy-start | bytes 6291460
  227.4 4.5 copy-start.2
  231.9 47.8 %copy-start.6 = (s32[768,128]{1,0:T(8,128)S(1)}, s32[768,128]{1,0:T(8,128)}, u32[]{:S(2)}) copy-start(s32[768,128]{1,0:T(8,128)} %param.11) | copy-start | bytes 1179652
  242.6 122.8 %all-reduce.11.cloned.1.call-start = ((), (), s32[]{:S(2)}) async-start(), calls=%async_computation.5 | async-start | bytes 4194304 | tf_op jit(solution)/shard_map/psum | solution.py:57
  303.7 115.4 %all-reduce.13.cloned.1.call-start = ((), (), s32[]{:S(2)}) async-start(), calls=%async_computation.6 | async-start | bytes 2097152 | tf_op jit(solution)/shard_map/psum | solution.py:11
  367.6 155.1 %all-reduce.15.cloned.1.call-start = ((), (), s32[]{:S(2)}) async-start(), calls=%async_computation.7 | async-start | bytes 4194304 | tf_op jit(solution)/shard_map/psum | solution.py:63
  461.6 111.3 %all-reduce.17.cloned.1.call-start = ((), (), s32[]{:S(2)}) async-start(), calls=%async_computation.8 | async-start | bytes 786432 | tf_op jit(solution)/shard_map/psum | solution.py:48
  536.7 122.8 %all-reduce.19.cloned.1.call-start = ((), (), s32[]{:S(2)}) async-start(), calls=%async_computation.9 | async-start | bytes 4194304 | tf_op jit(solution)/shard_map/psum | solution.py:57
  574.0 23.8 %copy-start.7 = (f32[768,128]{1,0:T(8,128)}, f32[768,128]{1,0:T(8,128)S(1)}, u32[]{:S(2)}) copy-start(f32[768,128]{1,0:T(8,128)S(1)} %divide_subtract_fusion) | copy-start | bytes 1179652
  597.8 115.5 %all-reduce.21.cloned.1.call-start = ((), (), s32[]{:S(2)}) async-start(), calls=%async_computation.10 | async-start | bytes 2097152 | tf_op jit(solution)/shard_map/psum | solution.py:11
  661.8 154.7 %all-reduce.23.cloned.1.call-start = ((), (), s32[]{:S(2)}) async-start(), calls=%async_computation.11 | async-start | bytes 4194304 | tf_op jit(solution)/shard_map/psum | solution.py:63
  816.5 6.9 copy-start.1
Sparse Core Ops, SparseCore 0:
  13.0 50.4 reduce-scatter.1
  65.0 49.3 all-gather.2
  116.3 70.7 all-gather.4
  242.7 36.9 all-reduce.8
  303.8 61.4 all-reduce.10
  368.2 50.9 all-reduce.12
  461.7 61.0 all-reduce.14
  536.8 36.0 all-reduce.16
  597.9 61.5 all-reduce.18
  662.3 50.9 all-reduce.20
  755.5 61.0 all-reduce.22
where the time goes:
time: 834 us; the launch traced here: 830 us
  waiting for transfers between devices  592 us (71%)
  matrix products  194 us (23%)
  other arithmetic  17.6 us (2%)
  between operations  14.2 us (2%)
  local copies, waits for them, and re-layouts  12.6 us (2%)
    psum x2, waiting for transfers between devices, on_device(): gradient = lax.psum(local_grad, 'row')  123 us
    psum x2, waiting for transfers between devices, on_device(): current = current - step_size * lax.psum(product_term, 'row')  120 us
    psum x2, waiting for transfers between devices, broadcast(): return lax.psum(block, axis)  103 us
    dot_general x2, matrix products, on_device(): jnp.dot(inverse_tiles, grad_block, precision=highest, preferred_element_t...  84.5 us
    psum x2, waiting for transfers between devices, on_device(): predicted = lax.psum(local_pred, 'col')  73.2 us
    all_gather x1, waiting for transfers between devices, on_device(): land_full = lax.all_gather(landmarks, 'row', axis=1, tiled=True)  70.6 us
    reduce_scatter x1, waiting for transfers between devices, on_device(): lax.psum_scatter(jnp.dot(documents, projection, precision=highest, prefer...  50.5 us
    all_gather x1, waiting for transfers between devices, on_device(): rows_in = lax.all_gather(proj_share, 'col', axis=0, tiled=True)  50.2 us
  transfers between devices with their start and end apart: 11, of which 11 were waited for; matrix products, arithmetic and copies ran while one was open for 0% of the time, Pallas kernels for 0%

commit v1 on v0

--- a/solution.py
+++ b/solution.py
@@ -22,7 +22,12 @@
         scatter_dimension=0,
         tiled=True,
     )
-    rows_in = lax.all_gather(proj_share, "col", axis=0, tiled=True)
+    ring = [proj_share]
+    for hop in range(3):
+        ring.append(lax.ppermute(ring[-1], "col", [(dev, (dev + 1) % 4) for dev in range(4)]))
+    rows_in = jnp.roll(
+        jnp.concatenate(ring[::-1], axis=0), (lax.axis_index("col") + 1) * ring[0].shape[0], axis=0
+    )
     sq_doc = jnp.sum(rows_in * rows_in, axis=1)
     inner = lax.dot_general(
         rows_in,

time: 834 us -> 760 us (0.911)
  waiting for transfers between devices: 592 us -> 511 us
    all_gather x1, waiting for transfers between devices: 70.6 us -> 0.03 us  [on_device(): land_full = lax.all_gather(landmarks, 'row', axis=1, tiled=True)]
    all_gather x1 -> x0, waiting for transfers between devices: 50.2 us -> none  [on_device(): rows_in = lax.all_gather(proj_share, 'col', axis=0, tiled=True)]
    ppermute x0 -> x3, waiting for transfers between devices: none -> 46.2 us  [on_device(): lax.ppermute(ring[-1], 'col', [(dev, (dev + 1) % 4) for dev in range(4)])]
  transfers between devices with their start and end apart: 11 -> 13, of which waited for: 11 -> 12; matrix products, arithmetic and copies ran while one was open for 0% -> 0% of each run, Pallas kernels for 0% -> 0%
where the time goes in v1:
time: 760 us; the launch traced here: 756 us
  waiting for transfers between devices  511 us (67%)
  matrix products  195 us (26%)
  local copies, waits for them, and re-layouts  16.1 us (2%)
  between operations  16.1 us (2%)
  other arithmetic  15.9 us (2%)
    psum x2, waiting for transfers between devices, on_device(): gradient = lax.psum(local_grad, 'row')  122 us
    psum x2, waiting for transfers between devices, on_device(): current = current - step_size * lax.psum(product_term, 'row')  119 us
    psum x2, waiting for transfers between devices, broadcast(): return lax.psum(block, axis)  103 us
    dot_general x2, matrix products, on_device(): jnp.dot(inverse_tiles, grad_block, precision=highest, preferred_element_t...  84.5 us
    psum x2, waiting for transfers between devices, on_device(): predicted = lax.psum(local_pred, 'col')  71.6 us
    reduce_scatter x1, waiting for transfers between devices, on_device(): lax.psum_scatter(jnp.dot(documents, projection, precision=highest, prefer...  49.9 us
    dot_general x2, matrix products, on_device(): lax.dot_general(kernel, residual, (((0,), (0,)), ((), ())), precision=hig...  47.6 us
    ppermute x3, waiting for transfers between devices, on_device(): lax.ppermute(ring[-1], 'col', [(dev, (dev + 1) % 4) for dev in range(4)])  46.2 us
  transfers between devices with their start and end apart: 13, of which 12 were waited for; matrix products, arithmetic and copies ran while one was open for 0% of the time, Pallas kernels for 0%

profile of v1, /device:TPU:0, one launch (start us, length us, event | category | flops | bytes accessed | tf_op | source)
XLA Modules:
  0.0 755.9 jit_solution(9313436606771070671)
XLA Ops:
  8.0 0.0 reduce-scatter.2.cloned.1.call-start
  8.1 1.0 copy-done
  9.1 4.6 fusion.13
  13.7 0.0 all-gather.2.cloned.1.call-start
  13.7 0.5 all-gather.2.cloned.1.call-update
  14.2 0.0 all-reduce.9.cloned.1.call-start
  14.3 49.9 %reduce-scatter.2.cloned.1.call-done = f32[192,768]{1,0:T(8,128)} async-done(((f32[768,768]{1,0:T(8,128)}), f32[192,768]{1,0:T(8,128)}) %reduce-scatter.2.cloned.1.call-update) | async-done | bytes 589840 | tf_op jit(solution)/shard_map/reduce_scatter | solution.py:19
  64.2 0.8 collective-permute-start
  65.1 15.8 %collective-permute-done = f32[192,768]{1,0:T(8,128)S(1)} collective-permute-done((f32[192,768]{1,0:T(8,128)}, f32[192,768]{1,0:T(8,128)S(1)}, u32[]{:S(2)}, u32[]{:S(2)}) %collective-permute-start) | collective-permute-done | bytes 589856 | tf_op jit(solution)/shard_map/ppermute | solution.py:27
  80.9 15.6 %collective-permute-done.1 = f32[192,768]{1,0:T(8,128)S(1)} collective-permute-done((f32[192,768]{1,0:T(8,128)S(1)}, f32[192,768]{1,0:T(8,128)S(1)}, u32[]{:S(2)}, u32[]{:S(2)}) %collective-permute-start.1) | collective-permute-done | bytes 589856 | tf_op jit(solution)/shard_map/ppermute | solution.py:27
  96.5 14.7 %collective-permute-done.2 = f32[192,768]{1,0:T(8,128)S(1)} collective-permute-done((f32[192,768]{1,0:T(8,128)S(1)}, f32[192,768]{1,0:T(8,128)S(1)}, u32[]{:S(2)}, u32[]{:S(2)}) %collective-permute-start.2) | collective-permute-done | bytes 589856 | tf_op jit(solution)/shard_map/ppermute | solution.py:27
  111.4 1.1 constant_dynamic-update-slice_fusion.4
  112.7 2.1 copy-done.6
  114.8 0.4 multiply_reduce_fusion.1
  115.2 0.0 all-gather.2.cloned.1.call-done
  115.2 5.9 multiply_reduce_fusion
  121.1 2.3 copy-done.3
  123.4 34.2 %multiply_exponential_fusion = f32[768,4096]{1,0:T(8,128)S(1)} fusion(f32[4096,768]{0,1:T(8,128)S(1)} %copy-done.3, f32[4096]{0:T(1024)S(1)} %multiply_reduce_fusion, f32[768]{0:T(1024)S(1)} %multiply_reduce_fusion.1, f32[1536,768]{1,0:T(8,128)} %copy-done.6, s32[]{:T(128)S(6)} %select_n.42), kind=kOutput, calls=%fused_computation | convolution fusion | flops 29003612160 | bytes 27544580 | tf_op jit(solution)/shard_map/dot_general | solution.py:32
  157.6 4.5 copy-done.2
  162.1 10.6 %fusion.14 = f32[768,128]{1,0:T(8,128)} fusion(f32[768,4096]{1,0:T(8,128)S(1)} %multiply_exponential_fusion, f32[4096,128]{1,0:T(8,128)S(1)} %copy-done.4), kind=kOutput, calls=%fused_computation.32 | convolution fusion | flops 4831838208 | bytes 15073280 | tf_op jit(solution)/shard_map/dot_general | solution.py:52
  172.8 0.0 all-reduce.11.cloned.1.call-start
  172.8 35.2 %all-reduce.9.cloned.1.call-done = f32[768,128]{1,0:T(8,128)} async-done(((f32[768,128]{1,0:T(8,128)}), f32[768,128]{1,0:T(8,128)}) %all-reduce.9.cloned.1.call-update) | async-done | bytes 393232 | tf_op jit(solution)/shard_map/psum | solution.py:53
  208.1 23.8 %fusion.2 = f32[4096,128]{1,0:T(8,128)} fusion(f32[768,4096]{1,0:T(8,128)} %copy-done.2, s32[768,128]{1,0:T(8,128)S(1)} %copy-done.7, f32[768,128]{1,0:T(8,128)} %all-reduce.9.cloned.1.call-done), kind=kOutput, calls=%fused_computation.12 | convolution fusion | flops 4832329728 | bytes 15466496 | tf_op jit(solution)/shard_map/dot_general | solution.py:55
  231.9 0.0 all-reduce.13.cloned.1.call-start
  232.0 60.8 %all-reduce.11.cloned.1.call-done = f32[4096,128]{1,0:T(8,128)} async-done(((f32[4096,128]{1,0:T(8,128)}), f32[4096,128]{1,0:T(8,128)}) %all-reduce.11.cloned.1.call-update) | async-done | bytes 2097168 | tf_op jit(solution)/shard_map/psum | solution.py:62
  292.7 2.3 dynamic-slice_select_fusion.1
  295.0 0.0 all-reduce.15.cloned.1.call-start
  295.1 51.3 %all-reduce.13.cloned.1.call-done = f32[2048,128]{1,0:T(8,128)} async-done(((f32[2048,128]{1,0:T(8,128)}), f32[2048,128]{1,0:T(8,128)}) %all-reduce.13.cloned.1.call-update) | async-done | bytes 1048592 | tf_op jit(solution)/shard_map/psum | solution.py:11
  346.3 42.4 %convolution_bitcast_fusion.1 = f32[4096,128]{0,1:T(8,128)} fusion(f32[2048,128]{1,0:T(8,128)} %all-reduce.13.cloned.1.call-done, f32[4096,2048]{1,0:T(8,128)} %param.10), kind=kOutput, calls=%fused_computation.3 | convolution fusion | flops 12884901888 | bytes 36700160 | tf_op jit(solution)/shard_map/dot_general | solution.py:65
  388.8 0.0 all-reduce.15.cloned.1.call-update
  388.8 0.0 all-reduce.17.cloned.1.call-start
  388.8 1.9 copy.8
  390.8 58.4 %all-reduce.15.cloned.1.call-done = f32[4096,128]{0,1:T(8,128)} async-done(((f32[4096,128]{0,1:T(8,128)}), f32[4096,128]{0,1:T(8,128)}) %all-reduce.15.cloned.1.call-update) | async-done | bytes 2097168 | tf_op jit(solution)/shard_map/psum | solution.py:68
  449.1 13.9 %fusion.1 = f32[768,128]{1,0:T(8,128)} fusion(f32[768,4096]{1,0:T(8,128)} %copy-done.2, f32[4096,128]{0,1:T(8,128)S(1)} %copy.8, f32[4096,128]{0,1:T(8,128)} %all-reduce.15.cloned.1.call-done), kind=kOutput, calls=%fused_computation.10 | convolution fusion | flops 4832886784 | bytes 17170432 | tf_op jit(solution)/shard_map/dot_general | solution.py:52
  463.1 0.0 all-reduce.19.cloned.1.call-start
  463.1 36.3 %all-reduce.17.cloned.1.call-done = f32[768,128]{1,0:T(8,128)} async-done(((f32[768,128]{1,0:T(8,128)}), f32[768,128]{1,0:T(8,128)}) %all-reduce.17.cloned.1.call-update) | async-done | bytes 393232 | tf_op jit(solution)/shard_map/psum | solution.py:53
  499.4 1.1 divide_subtract_fusion
  500.6 23.8 %fusion.15 = f32[4096,128]{1,0:T(8,128)} fusion(f32[768,4096]{1,0:T(8,128)} %copy-done.2, f32[768,128]{1,0:T(8,128)S(1)} %divide_subtract_fusion), kind=kOutput, calls=%fused_computation.33 | convolution fusion | flops 4831838208 | bytes 15073280 | tf_op jit(solution)/shard_map/dot_general | solution.py:55
  524.4 0.0 all-reduce.19.cloned.1.call-update
  524.4 0.0 all-reduce.21.cloned.1.call-start
  524.4 60.8 %all-reduce.19.cloned.1.call-done = f32[4096,128]{1,0:T(8,128)} async-done(((f32[4096,128]{1,0:T(8,128)}), f32[4096,128]{1,0:T(8,128)}) %all-reduce.19.cloned.1.call-update) | async-done | bytes 2097168 | tf_op jit(solution)/shard_map/psum | solution.py:62
  585.2 2.3 dynamic-slice_select_fusion
  587.5 0.0 all-reduce.23.cloned.1.call-start
  587.6 51.3 %all-reduce.21.cloned.1.call-done = f32[2048,128]{1,0:T(8,128)} async-done(((f32[2048,128]{1,0:T(8,128)}), f32[2048,128]{1,0:T(8,128)}) %all-reduce.21.cloned.1.call-update) | async-done | bytes 1048592 | tf_op jit(solution)/shard_map/psum | solution.py:11
  638.8 42.1 %convolution_bitcast_fusion = f32[4096,128]{0,1:T(8,128)} fusion(f32[2048,128]{1,0:T(8,128)} %all-reduce.21.cloned.1.call-done, f32[4096,2048]{1,0:T(8,128)} %param.10), kind=kOutput, calls=%fused_computation.2 | convolution fusion | flops 12884901888 | bytes 36700160 | tf_op jit(solution)/shard_map/dot_general | solution.py:65
  680.9 60.3 %all-reduce.23.cloned.1.call-done = f32[4096,128]{0,1:T(8,128)} async-done(((f32[4096,128]{0,1:T(8,128)}), f32[4096,128]{0,1:T(8,128)}) %all-reduce.23.cloned.1.call-update) | async-done | bytes 2097168 | tf_op jit(solution)/shard_map/psum | solution.py:68
  741.3 4.0 multiply_subtract_fusion
  745.3 2.9 copy.9
  (30 shorter events, 0.4 us)
Async XLA Ops:
  8.0 1.1 copy-start
  8.0 56.2 %reduce-scatter.2.cloned.1.call-start = ((), (), s32[]{:S(2)}) async-start(), calls=%async_computation.1 | async-start | bytes 2949120 | tf_op jit(solution)/shard_map/reduce_scatter | solution.py:19
  13.7 101.6 %all-gather.2.cloned.1.call-start = ((), (), s32[]{:S(2)}) async-start(), calls=%async_computation.2 | async-start | bytes 14155776 | tf_op jit(solution)/shard_map/all_gather | solution.py:16
  14.2 193.8 %all-reduce.9.cloned.1.call-start = ((), (), s32[]{:S(2)}) async-start(), calls=%async_computation.3 | async-start | bytes 786432 | tf_op jit(solution)/shard_map/psum | solution.py:53
  64.2 48.4 %copy-start.5 = (f32[192,768]{1,0:T(8,128)S(1)}, f32[192,768]{1,0:T(8,128)}, u32[]{:S(2)}) copy-start(f32[192,768]{1,0:T(8,128)} %reduce-scatter.2.cloned.1.call-done) | copy-start | bytes 1769476
  64.2 16.7 %collective-permute-start = (f32[192,768]{1,0:T(8,128)}, f32[192,768]{1,0:T(8,128)S(1)}, u32[]{:S(2)}, u32[]{:S(2)}) collective-permute-start(f32[192,768]{1,0:T(8,128)} %reduce-scatter.2.cloned.1.call-done), channel_id=1, source_target_pairs={{0,1},{1,2},{2,3},{3,0},{4,5},{5,6},{6,7},{7,4},{8,9},{9,10},{10,1... | collective-permute-start | bytes 1769480 | tf_op jit(solution)/shard_map/ppermute | solution.py:27
  80.9 15.6 %collective-permute-start.1 = (f32[192,768]{1,0:T(8,128)S(1)}, f32[192,768]{1,0:T(8,128)S(1)}, u32[]{:S(2)}, u32[]{:S(2)}) collective-permute-start(f32[192,768]{1,0:T(8,128)S(1)} %collective-permute-done), channel_id=1, source_target_pairs={{0,1},{1,2},{2,3},{3,0},{4,5},{5,6},{6,7},{7,4},{8,9},{9,10},{10,1... | collective-permute-start | bytes 1769480 | tf_op jit(solution)/shard_map/ppermute | solution.py:27
  96.5 14.7 %collective-permute-start.2 = (f32[192,768]{1,0:T(8,128)S(1)}, f32[192,768]{1,0:T(8,128)S(1)}, u32[]{:S(2)}, u32[]{:S(2)}) collective-permute-start(f32[192,768]{1,0:T(8,128)S(1)} %collective-permute-done.1), channel_id=1, source_target_pairs={{0,1},{1,2},{2,3},{3,0},{4,5},{5,6},{6,7},{7,4},{8,9},{9,10},{10,1... | collective-permute-start | bytes 1769480 | tf_op jit(solution)/shard_map/ppermute | solution.py:27
  112.7 2.1 copy-start.6
  115.2 8.2 %copy-start.3 = (f32[4096,768]{0,1:T(8,128)S(1)}, f32[4096,768]{0,1:T(8,128)}, u32[]{:S(2)}) copy-start(f32[4096,768]{0,1:T(8,128)} %all-gather.2.cloned.1.call-done) | copy-start | bytes 37748740
  123.4 38.8 %copy-start.4 = (f32[4096,128]{1,0:T(8,128)S(1)}, f32[4096,128]{1,0:T(8,128)}, u32[]{:S(2)}) copy-start(f32[4096,128]{1,0:T(8,128)} %param.9) | copy-start | bytes 6291460
  157.6 4.5 copy-start.2
  162.1 45.9 %copy-start.7 = (s32[768,128]{1,0:T(8,128)S(1)}, s32[768,128]{1,0:T(8,128)}, u32[]{:S(2)}) copy-start(s32[768,128]{1,0:T(8,128)} %param.11) | copy-start | bytes 1179652
  172.8 119.9 %all-reduce.11.cloned.1.call-start = ((), (), s32[]{:S(2)}) async-start(), calls=%async_computation.4 | async-start | bytes 4194304 | tf_op jit(solution)/shard_map/psum | solution.py:62
  231.9 114.4 %all-reduce.13.cloned.1.call-start = ((), (), s32[]{:S(2)}) async-start(), calls=%async_computation.5 | async-start | bytes 2097152 | tf_op jit(solution)/shard_map/psum | solution.py:11
  295.0 154.1 %all-reduce.15.cloned.1.call-start = ((), (), s32[]{:S(2)}) async-start(), calls=%async_computation.6 | async-start | bytes 4194304 | tf_op jit(solution)/shard_map/psum | solution.py:68
  388.8 110.6 %all-reduce.17.cloned.1.call-start = ((), (), s32[]{:S(2)}) async-start(), calls=%async_computation.7 | async-start | bytes 786432 | tf_op jit(solution)/shard_map/psum | solution.py:53
  463.1 122.2 %all-reduce.19.cloned.1.call-start = ((), (), s32[]{:S(2)}) async-start(), calls=%async_computation.8 | async-start | bytes 4194304 | tf_op jit(solution)/shard_map/psum | solution.py:62
  500.5 23.8 %copy-start.8 = (f32[768,128]{1,0:T(8,128)}, f32[768,128]{1,0:T(8,128)S(1)}, u32[]{:S(2)}) copy-start(f32[768,128]{1,0:T(8,128)S(1)} %divide_subtract_fusion) | copy-start | bytes 1179652
  524.4 114.4 %all-reduce.21.cloned.1.call-start = ((), (), s32[]{:S(2)}) async-start(), calls=%async_computation.9 | async-start | bytes 2097152 | tf_op jit(solution)/shard_map/psum | solution.py:11
  587.5 153.8 %all-reduce.23.cloned.1.call-start = ((), (), s32[]{:S(2)}) async-start(), calls=%async_computation.10 | async-start | bytes 4194304 | tf_op jit(solution)/shard_map/psum | solution.py:68
  680.9 67.2 %copy-start.1 = (f32[768,192]{0,1:T(8,128)S(1)}, f32[768,192]{0,1:T(8,128)}, u32[]{:S(2)}) copy-start(f32[768,192]{0,1:T(8,128)} %param.6) | copy-start | bytes 1769476
Sparse Core Ops, SparseCore 0:
  13.8 50.4 reduce-scatter.1
  172.9 35.1 all-reduce.8
  295.1 51.1 all-reduce.12
  463.2 36.2 all-reduce.16
  587.6 51.1 all-reduce.20
Sparse Core Ops, SparseCore 1:
  16.0 74.6 all-gather.1
  232.0 60.7 all-reduce.10
  388.9 60.2 all-reduce.14
  524.5 60.7 all-reduce.18
  681.0 60.2 all-reduce.22
